TPU v7x, 128 devices: a whole 4x4x4 slice. The times are simulated.
128 devices in a mesh: sec: 2 (over y_lo), dev: 64 (over x, y_hi, z, core).
Axes of the slice: x: 4, y: 4 (y_hi: 2, y_lo: 2; y = y_hi * 2 + y_lo), z: 4, core: 2. Of those that a mesh axis runs over, the one named last changes fastest.
Arguments:
- hidden_in: bfloat16 [2048, 7168], P(('sec', 'dev')), may hold values from -6 to 6
- expert_ids: int32 [2048, 8], P(('sec', 'dev')), may hold values from 0 to 63, all different within a row; in each aligned block of 8 rows (0 to 7, 8 to 15, ...) at most 2 rows name the same one
- gate_coef: float32 [2048, 8], P(('sec', 'dev')), may hold values from 0.1 to 1
- query_lat: bfloat16 [2048, 64, 576], P(('sec', 'dev')), may hold values from -40 to 40
- kv_cache: bfloat16 [2048, 128, 576], P(('sec', 'dev')), may hold values from -6 to 6
- cache_len: int32 [2048], P(('sec', 'dev')), may hold values from 32 to 128, as said below
- gate_weight: bfloat16 [64, 7168, 1024], P('dev', None, 'sec'), may hold values from -0.0625 to 0.0625
- up_weight: bfloat16 [64, 7168, 1024], P('dev', None, 'sec'), may hold values from -0.0625 to 0.0625
- down_weight: bfloat16 [64, 1024, 7168], P('dev', 'sec'), may hold values from -0.1875 to 0.1875
Outputs:
- attention: bfloat16 [2048, 64, 512], P(('sec', 'dev'))
- routed_out: bfloat16 [2048, 7168], P(('sec', 'dev'))
Inputs may be any that keep to these rules, and one draw needn't show every extreme that they name: `expert_ids`: each row names 8 different experts. In each aligned block of 8 rows (one micro-batch of one device) no expert is named by more than 2 rows, and in some block an expert is named by exactly 2 rows. `cache_len`: some row uses all 128 slots.
All inputs are finite; a program needn't handle non-finite values.
Results may differ from a plain program's by a relative error of at most 0.0065.
Values may be sent and summed in bfloat16 or wider, within the bound.
A program may use at most 128 MiB of HBM per device.

v0:
```python
import math

import jax
import jax.numpy as jnp
from jax import lax
from jax.sharding import PartitionSpec as P

LAT = 512
TOP = 8


score_scale = 1.0 / math.sqrt(192.0)


def attend(query_lat, kv_cache, cache_len):
    scores = (
        jnp.einsum("rhk,rlk->rhl", query_lat, kv_cache, preferred_element_type=jnp.float32)
        * score_scale
    )
    positions = jnp.arange(kv_cache.shape[1], dtype=jnp.int32)
    visible = positions[None, None, :] < cache_len[:, None, None]
    scores = jnp.where(visible, scores, jnp.float32(-1e30))
    top_score = jnp.max(scores, axis=2, keepdims=True)
    exponent = jnp.exp(scores - top_score)
    denominator = jnp.sum(exponent, axis=2, keepdims=True)
    weights = (exponent / denominator).astype(jnp.bfloat16)
    return jnp.einsum(
        "rhl,rlc->rhc", weights, kv_cache[:, :, :LAT], preferred_element_type=jnp.float32
    ).astype(jnp.bfloat16)


def routing_tables(expert_ids, gate_coef, expert_count, capacity):
    row_count, top_count = expert_ids.shape
    flat_ids = expert_ids.reshape(-1)
    position_ids = jnp.arange(flat_ids.shape[0], dtype=jnp.int32)
    matches = (flat_ids[:, None] == flat_ids[None, :]) & (
        position_ids[None, :] < position_ids[:, None]
    )
    slot_rank = jnp.sum(matches.astype(jnp.int32), axis=1)
    target = flat_ids * capacity + slot_rank
    slot_ids = jnp.arange(expert_count * capacity, dtype=jnp.int32)
    placed = (target[None, :] == slot_ids[:, None]).astype(jnp.float32)
    owner_hot = (
        (position_ids // top_count)[:, None] == jnp.arange(row_count, dtype=jnp.int32)[None, :]
    ).astype(jnp.float32)
    picker = jnp.dot(placed, owner_hot, precision=lax.Precision.HIGHEST).astype(jnp.bfloat16)
    weighted = owner_hot * gate_coef.reshape(-1)[:, None]
    mixing = jnp.dot(weighted.T, placed.T, precision=lax.Precision.HIGHEST)
    return (picker, mixing)


def expert_rows(tokens, gate_weight, up_weight, down_weight):
    shape_in = tokens.shape
    flat_rows = tokens.reshape(-1, shape_in[-1])
    gate_val = jnp.dot(flat_rows, gate_weight[0], preferred_element_type=jnp.float32)
    up_val = jnp.dot(flat_rows, up_weight[0], preferred_element_type=jnp.float32)
    hidden = (jax.nn.silu(gate_val) * up_val).astype(jnp.bfloat16)
    part_out = jnp.dot(hidden, down_weight[0], preferred_element_type=jnp.float32).astype(
        jnp.bfloat16
    )
    return part_out.reshape(shape_in)


def route_tokens(send_buf, gate_weight, up_weight, down_weight):
    section_count = lax.axis_size("sec")
    doubled = jnp.concatenate([send_buf] * section_count, axis=0)
    halves = expert_rows(
        lax.all_to_all(doubled, ("sec", "dev"), split_axis=0, concat_axis=0, tiled=True),
        gate_weight,
        up_weight,
        down_weight,
    )
    returned = lax.all_to_all(halves, ("sec", "dev"), split_axis=0, concat_axis=0, tiled=True)
    pieces = returned.reshape((section_count,) + send_buf.shape).astype(jnp.float32)
    return jnp.sum(pieces, axis=0).astype(jnp.bfloat16)


def combine(returned, mixing):
    flat_back = returned.reshape(-1, returned.shape[-1]).astype(jnp.float32)
    return jnp.dot(mixing, flat_back, precision=lax.Precision.HIGHEST).astype(jnp.bfloat16)


def per_device(
    hidden_in,
    expert_ids,
    gate_coef,
    query_lat,
    kv_cache,
    cache_len,
    gate_weight,
    up_weight,
    down_weight,
):
    half_rows = hidden_in.shape[0] // 2
    model_width = hidden_in.shape[1]
    expert_count = lax.axis_size("dev")
    capacity = max(2, 2 * TOP * half_rows // expert_count)
    tables = []
    send_bufs = []
    for offset in (0, half_rows):
        picker, mixing = routing_tables(
            expert_ids[offset : offset + half_rows],
            gate_coef[offset : offset + half_rows],
            expert_count,
            capacity,
        )
        tables.append(mixing)
        gathered = jnp.dot(
            picker, hidden_in[offset : offset + half_rows], preferred_element_type=jnp.float32
        ).astype(jnp.bfloat16)
        send_bufs.append(gathered.reshape(expert_count, capacity, model_width))
    attention = attend(query_lat, kv_cache, cache_len)
    joined = jnp.concatenate(send_bufs, axis=1)
    returned = route_tokens(joined, gate_weight, up_weight, down_weight)
    first_back = returned[:, :capacity]
    second_back = returned[:, capacity:]
    routed_out = jnp.concatenate(
        [combine(first_back, tables[0]), combine(second_back, tables[1])], axis=0
    )
    return (attention, routed_out)


def solution(mesh):
    in_specs = (
        P(("sec", "dev"), None),
        P(("sec", "dev"), None),
        P(("sec", "dev"), None),
        P(("sec", "dev"), None, None),
        P(("sec", "dev"), None, None),
        P(("sec", "dev")),
        P("dev", None, "sec"),
        P("dev", None, "sec"),
        P("dev", "sec", None),
    )
    out_specs = (P(("sec", "dev"), None, None), P(("sec", "dev"), None))
    return jax.shard_map(
        per_device, mesh=mesh, in_specs=in_specs, out_specs=out_specs, check_vma=False
    )
```

profile of v0, /device:TPU:23, one launch (start us, length us, event | category | flops | bytes accessed | tf_op | source)
XLA Modules:
  0.0 305.9 jit_solution(1223711301129978982)
XLA Ops:
  0.6 0.0 copy-start
  0.6 0.9 fusion.46
  1.5 0.1 copy.19
  1.6 0.1 reshape.91
  1.7 0.2 convert_reduce_fusion
  1.9 0.2 convolution_convert_fusion.5
  2.1 1.5 convolution_convert_fusion.1
  3.6 1.7 reshape.92
  5.3 0.1 copy.18
  5.3 0.1 reshape.89
  5.4 0.2 convert_reduce_fusion.1
  5.6 0.2 convolution_convert_fusion.6
  5.8 1.5 convolution_convert_fusion.2
  7.3 1.7 reshape.90
  9.0 9.5 %maximum_maximum_fusion = bf16[128,4,7168]{2,1,0:T(4,128)(2,1)S(1)} fusion(bf16[64,2,7168]{2,1,0:T(2,128)(2,1)} %reshape.92, bf16[64,2,7168]{2,1,0:T(2,128)(2,1)} %reshape.90), kind=kLoop, calls=%fused_computation.6 | loop fusion | flops 29360128 | bytes 11010048 | tf_op jit(solution)/shard_map/concatenate | solution.py:66
  18.5 97.7 %all_to_all.10 = bf16[128,4,7168]{2,1,0:T(4,128)(2,1)} all-to-all(bf16[128,4,7168]{2,1,0:T(4,128)(2,1)S(1)} %maximum_maximum_fusion), channel_id=1, replica_groups=mesh['sec'=2,'dev'=64] {'sec','dev'}, dimensions={0} | all-to-all | bytes 14680064 | tf_op jit(solution)/shard_map/all_to_all | solution.py:68
  116.2 12.1 %reshape.93 = bf16[512,7168]{1,0:T(8,128)(2,1)} reshape(bf16[128,4,7168]{2,1,0:T(4,128)(2,1)} %all_to_all.10) | data formatting | bytes 14680064 | tf_op jit(solution)/shard_map/reshape | solution.py:54
  128.3 0.0 copy-start.1
  128.3 9.3 %fusion.4 = f32[512,512]{1,0:T(8,128)S(1)} fusion(bf16[512,7168]{1,0:T(8,128)(2,1)} %reshape.93, bf16[1,7168,512]{2,1,0:T(8,128)(2,1)} %param.15), kind=kOutput, calls=%fused_computation.10 | convolution fusion | flops 3758096384 | bytes 15728640 | tf_op jit(solution)/shard_map/dot_general | solution.py:55
  137.6 0.0 copy-done.1
  137.6 7.2 %fusion.14 = bf16[512,512]{1,0:T(8,128)(2,1)S(1)} fusion(bf16[512,7168]{1,0:T(8,128)(2,1)S(1)} %copy-done.1, bf16[1,7168,512]{2,1,0:T(8,128)(2,1)} %param.16, f32[512,512]{1,0:T(8,128)S(1)} %fusion.4), kind=kOutput, calls=%fused_computation.16 | convolution fusion | flops 3759669248 | bytes 16252928 | tf_op jit(solution)/shard_map/dot_general | solution.py:56
  144.8 9.3 %convolution_convert_fusion = bf16[512,7168]{1,0:T(8,128)(2,1)} fusion(bf16[512,512]{1,0:T(8,128)(2,1)S(1)} %fusion.14, bf16[1,512,7168]{2,1,0:T(8,128)(2,1)} %param.17), kind=kOutput, calls=%fused_computation.1 | convolution fusion | flops 3761766400 | bytes 15204352 | tf_op jit(solution)/shard_map/dot_general | solution.py:58
  154.1 12.6 %reshape.94 = bf16[128,4,7168]{2,1,0:T(4,128)(2,1)} reshape(bf16[512,7168]{1,0:T(8,128)(2,1)} %convolution_convert_fusion) | data formatting | bytes 14680064 | tf_op jit(solution)/shard_map/reshape | solution.py:61
  166.7 0.0 copy-start.2
  166.7 0.0 copy-start.3
  166.7 11.1 %all-to-all-start.1 = ((bf16[128,4,7168]{2,1,0:T(4,128)(2,1)}), bf16[128,4,7168]{2,1,0:T(4,128)(2,1)}, u32[]{:S(2)}, u32[]{:S(2)}) async-start(bf16[128,4,7168]{2,1,0:T(4,128)(2,1)} %reshape.94), calls=%async_computation.1 | async-start | bytes 14680064 | tf_op jit(solution)/shard_map/all_to_all | solution.py:73
  177.8 0.0 copy-done.2
  177.8 0.1 fusion.45
  177.9 0.1 copy.17
  178.0 0.1 mul.49
  178.0 0.1 copy.20
  178.1 0.1 mul.56
  178.2 0.0 copy-done.3
  178.2 0.1 iota_compare_fusion.12
  178.3 0.0 copy-done
  178.3 2.3 fusion.19
  180.6 0.3 fusion.47
  180.9 0.2 fusion.24
  181.2 0.3 fusion.23
  181.5 4.5 %fusion.8 = bf16[16,64,512]{2,1,0:T(8,128)(2,1)} fusion(bf16[16,128,576]{1,2,0:T(8,128)(2,1)} %param.13, f32[16,64]{1,0:T(8,128)S(1)} %fusion.47, f32[16,64,128]{2,1,0:T(8,128)S(1)} %fusion.19), kind=kOutput, calls=%fused_computation.14 | convolution fusion | flops 135136384 | bytes 4202496 | tf_op jit(solution)/shard_map/rhl,rlc->rhc/dot_general | solution.py:27
  186.0 89.4 %all-to-all-done.1 = bf16[128,4,7168]{2,1,0:T(4,128)(2,1)} async-done(((bf16[128,4,7168]{2,1,0:T(4,128)(2,1)}), bf16[128,4,7168]{2,1,0:T(4,128)(2,1)}, u32[]{:S(2)}, u32[]{:S(2)}) %all-to-all-start.1) | async-done | bytes 7340064 | tf_op jit(solution)/shard_map/all_to_all | solution.py:73
  275.4 10.9 %reduce_sum.42 = bf16[64,4,7168]{2,1,0:T(4,128)(2,1)} reduce(bf16[2,64,4,7168]{3,2,1,0:T(4,128)(2,1)} %bitcast.3, bf16[]{:T(256)} %constant.37.clone.1), dimensions={0}, to_apply=%region_4.5 | reduce | flops 1835008 | bytes 11010050 | tf_op jit(solution)/shard_map/reduce_sum | solution.py:75
  286.3 7.6 %fusion.44 = (bf16[64,2,7168]{2,1,0:T(2,128)(2,1)}, bf16[64,2,7168]{2,1,0:T(2,128)(2,1)S(1)}) fusion(bf16[64,4,7168]{2,1,0:T(4,128)(2,1)} %reduce_sum.42), kind=kLoop, calls=%fused_computation.62 | loop fusion | bytes 7340032 | tf_op jit(solution)/shard_map/slice | solution.py:115
  293.9 4.9 %reshape.96 = bf16[128,7168]{1,0:T(8,128)(2,1)} reshape(bf16[64,2,7168]{2,1,0:T(2,128)(2,1)} %get-tuple-element.2) | data formatting | bytes 3670016 | tf_op jit(solution)/shard_map/reshape | solution.py:79
  298.8 1.7 reshape.97
  300.5 2.3 convolution_convert_fusion.4
  302.8 2.3 convolution_convert_fusion.3
  305.1 0.7 pad_maximum_fusion
  (2 shorter events, 0.0 us)
Async XLA Ops:
  0.6 177.6 %copy-start = (bf16[16,64,576]{2,1,0:T(8,128)(2,1)S(1)}, bf16[16,64,576]{2,1,0:T(8,128)(2,1)}, u32[]{:S(2)}) copy-start(bf16[16,64,576]{2,1,0:T(8,128)(2,1)} %param.12) | copy-start | bytes 3538948
  128.3 9.3 %copy-start.1 = (bf16[512,7168]{1,0:T(8,128)(2,1)S(1)}, bf16[512,7168]{1,0:T(8,128)(2,1)}, u32[]{:S(2)}) copy-start(bf16[512,7168]{1,0:T(8,128)(2,1)} %reshape.93) | copy-start | bytes 22020100
  166.7 11.1 %copy-start.2 = (f32[16,8]{0,1:T(8,128)S(1)}, f32[16,8]{0,1:T(8,128)}, u32[]{:S(2)}) copy-start(f32[16,8]{0,1:T(8,128)} %param.11) | copy-start | bytes 1540
  166.7 11.5 %copy-start.3 = (s32[16]{0:T(128)S(1)}, s32[16]{0:T(128)}, u32[]{:S(2)}) copy-start(s32[16]{0:T(128)} %param.14) | copy-start | bytes 196
  166.7 108.6 %all-to-all-start.1 = ((bf16[128,4,7168]{2,1,0:T(4,128)(2,1)}), bf16[128,4,7168]{2,1,0:T(4,128)(2,1)}, u32[]{:S(2)}, u32[]{:S(2)}) async-start(bf16[128,4,7168]{2,1,0:T(4,128)(2,1)} %reshape.94), calls=%async_computation.1 | async-start | bytes 14680064 | tf_op jit(solution)/shard_map/all_to_all | solution.py:73
where the time goes:
time: 307 us; the launch traced here: 306 us
  blocking collectives  97.7 us (32%)
  waiting for transfers between devices  89.4 us (29%)
  local copies, waits for them, and re-layouts  43.9 us (14%)
  matrix products  41.2 us (13%)
  other arithmetic  21.9 us (7%)
  starting transfers between devices  11.1 us (4%)
    all_to_all x1, blocking collectives, route_tokens(): lax.all_to_all(doubled, ('sec', 'dev'), split_axis=0, concat_axis=0, tile...  97.7 us
    all_to_all x1, waiting for transfers between devices, route_tokens(): lax.all_to_all(halves, ('sec', 'dev'), split_axis=0, concat_axis=0, tiled...  89.4 us
    reshape x1, local copies, waits for them, and re-layouts, expert_rows(): return part_out.reshape(shape_in)  12.6 us
    reshape x1, local copies, waits for them, and re-layouts, expert_rows(): flat_rows = tokens.reshape(-1, shape_in[-1])  12.1 us
    all_to_all x1, starting transfers between devices, route_tokens(): lax.all_to_all(halves, ('sec', 'dev'), split_axis=0, concat_axis=0, tiled...  11.1 us
    reduce_sum x1, other arithmetic, route_tokens(): return jnp.sum(pieces, axis=0).astype(jnp.bfloat16)  10.9 us
    concatenate x1, other arithmetic, route_tokens(): doubled = jnp.concatenate([send_buf] * section_count, axis=0)  9.5 us
    dot_general x1, matrix products, expert_rows(): jnp.dot(hidden, down_weight[0], preferred_element_type=jnp.float32)  9.3 us
  transfers between devices with their start and end apart: 1, of which 1 were waited for; matrix products, arithmetic and copies ran while one was open for 3% of the time, Pallas kernels for 0%

commit v1 on v0

v1 whole, which is shorter than its diff:
```python
import functools
import math

import jax
import jax.numpy as jnp
from jax import lax
from jax.experimental import pallas as pl
from jax.experimental.pallas import tpu as pltpu
from jax.sharding import PartitionSpec as P

LAT = 512
TOP = 8
MESH = pl.DeviceIdType.MESH
SCALE = 1.0 / math.sqrt(192.0)

WIDTHS = (2304, 2560, 2304)
OFFSETS = (0, 2304, 4864)
STEPS = (768, 1280, 768)
HALVES = (1152, 1280, 1152)
ORDERS = ((0, 1, 2), (2, 0, 1), (1, 2, 0))
TABLE = 128
LANES = 256


def iota(shape, dim):
    return lax.broadcasted_iota(jnp.int32, shape, dim)


def dot(a, b):
    return jnp.dot(a, b, preferred_element_type=jnp.float32)


def dot_nt(a, b):
    return lax.dot_general(a, b, (((1,), (1,)), ((), ())), preferred_element_type=jnp.float32)


def kernel(
    len_ref,
    ids_ref,
    coef_ref,
    hidden_ref,
    query_ref,
    cache_ref,
    gate_ref,
    up_ref,
    down_ref,
    att_ref,
    out_ref,
    *scratch,
):
    rows_buf = scratch[0:3]
    slot_buf = scratch[3:6]
    recv_buf = scratch[6:9]
    back_buf = scratch[9:12]
    relay_in = scratch[12:15]
    relay_out = scratch[15:18]
    part_buf = scratch[18:21]
    wide_a = scratch[21:24]
    wide_b = scratch[24:27]
    wide_c = scratch[27:30]
    wide_d = scratch[30:33]
    thin_a = scratch[33:36]
    thin_b = scratch[36:39]
    thin_c = scratch[39:42]
    thin_d = scratch[42:45]
    (gate_buf, up_buf, down_buf, acc, hid, hid_p, q_buf, kv_buf, o_buf) = scratch[45:54]
    send_sem, recv_sem, load_sem, own_sem, q_sem, kv_sem, o_sem = scratch[54:]

    sec = lax.axis_index("sec")
    dev = lax.axis_index("dev")
    core = dev % 2
    pos = (dev // 16, ((dev // 8) % 2) * 2 + sec, (dev // 2) % 4)

    def device(point, which):
        x, y, z = point
        return (y % 2, ((x * 2 + y // 2) * 4 + z) * 2 + which)

    def moved(dim, delta):
        point = list(pos)
        point[dim] = (pos[dim] + delta) % 4
        return tuple(point)

    turn = 1 - 2 * core
    pair = 1 - 2 * (pos[1] % 2)

    loads = [
        pltpu.make_async_copy(gate_ref.at[0], gate_buf, load_sem.at[0]),
        pltpu.make_async_copy(up_ref.at[0], up_buf, load_sem.at[1]),
        pltpu.make_async_copy(down_ref.at[0], down_buf, load_sem.at[2]),
    ]
    own = []
    for p in range(3):
        d1, d2, _ = ORDERS[p]
        own.append(
            pltpu.make_async_copy(
                hidden_ref.at[:, pl.ds(OFFSETS[p], WIDTHS[p])],
                rows_buf[p].at[pos[d1], pos[d2], :, pl.ds(0, WIDTHS[p])],
                own_sem.at[p],
            )
        )
        own[p].start()

    barrier = pltpu.get_barrier_semaphore()
    partners = [device(pos, 1 - core)]
    for dim in range(3):
        for delta in (1, -1):
            for which in range(2):
                partners.append(device(moved(dim, delta), which))
    for partner in partners:
        pl.semaphore_signal(barrier, inc=1, device_id=partner, device_id_type=MESH)

    lane = iota((16, TABLE), 1)
    hit = jnp.zeros((16, TABLE), jnp.float32)
    weight = jnp.zeros((16, TABLE), jnp.float32)
    for k in range(TOP):
        match = ids_ref[:, k : k + 1] == lane // 2
        hit = hit + jnp.where(match, 1.0, 0.0)
        weight = weight + jnp.where(match, coef_ref[:, k : k + 1], 0.0)
    low = (iota((16, 16), 1) < iota((16, 16), 0)) & (iota((16, 16), 1) // 8 == iota((16, 16), 0) // 8)
    rank = dot(jnp.where(low, 1.0, 0.0).astype(jnp.bfloat16), hit.astype(jnp.bfloat16))
    table = jnp.where(rank == (lane % 2).astype(jnp.float32), weight, 0.0).astype(jnp.bfloat16)
    for p in range(3):
        d1, d2, _ = ORDERS[p]
        rows_buf[p][pos[d1], pos[d2], :, pl.ds(WIDTHS[p], TABLE)] = table

    for p in range(3):
        own[p].wait()
    pl.semaphore_wait(barrier, len(partners))

    def remote(src, dst, p, send, recv, target):
        return pltpu.make_async_remote_copy(
            src_ref=src,
            dst_ref=dst,
            send_sem=send_sem.at[p, send],
            recv_sem=recv_sem.at[p, recv],
            device_id=target,
            device_id_type=MESH,
        )

    def arrived(dst, p, recv):
        remote(dst, dst, p, 0, recv, device(pos, 1 - core)).wait_recv()

    def q_copy(step, slot):
        return pltpu.make_async_copy(query_ref.at[pl.ds(step * 2, 2)], q_buf.at[slot], q_sem.at[slot])

    def kv_copy(step, slot):
        return pltpu.make_async_copy(cache_ref.at[pl.ds(step * 2, 2)], kv_buf.at[slot], kv_sem.at[slot])

    def o_copy(step, slot):
        return pltpu.make_async_copy(o_buf.at[slot], att_ref.at[pl.ds(step * 2, 2)], o_sem.at[slot])

    def attend(step, carry):
        slot = step % 2
        q_copy(step, slot).wait()
        kv_copy(step, slot).wait()

        @pl.when(step >= 2)
        def _():
            o_copy(step, slot).wait()

        for i in range(2):
            keys = kv_buf[slot, i]
            scores = dot_nt(q_buf[slot, i], keys) * SCALE
            visible = iota((64, 128), 1) < len_ref[step * 2 + i]
            scores = jnp.where(visible, scores, -1e30)
            exponent = jnp.exp(scores - jnp.max(scores, axis=1, keepdims=True))
            weights = (exponent / jnp.sum(exponent, axis=1, keepdims=True)).astype(jnp.bfloat16)
            o_buf[slot, i] = dot(weights, keys[:, :LAT]).astype(jnp.bfloat16)
        o_copy(step, slot).start()

        @pl.when(step + 2 < 8)
        def _():
            q_copy(step + 2, slot).start()
            kv_copy(step + 2, slot).start()

        return carry

    for step in range(2):
        q_copy(step, step).start()
        kv_copy(step, step).start()

    def ring(p, dim, base, block):
        half = HALVES[p]
        rest = WIDTHS[p] + TABLE - half
        here, up, down = pos[dim], (pos[dim] + 1) % 4, (pos[dim] + 3) % 4
        above, below = device(moved(dim, 1), core), device(moved(dim, -1), core)
        first = [
            remote(block(here), block(here), p, base, base, above),
            remote(block(here), block(here), p, base + 1, base + 1, below),
        ]
        low_part = lambda i: block(i, pl.ds(0, half))
        high_part = lambda i: block(i, pl.ds(half, rest))
        second = [
            remote(low_part(down), low_part(down), p, base + 2, base + 2, above),
            remote(high_part(up), high_part(up), p, base + 3, base + 3, below),
        ]
        far = (pos[dim] + 2) % 4
        waits = [
            lambda: arrived(block(down), p, base),
            lambda: arrived(block(up), p, base + 1),
            lambda: arrived(low_part(far), p, base + 2),
            lambda: arrived(high_part(far), p, base + 3),
        ]
        return first, second, waits

    rings_one, rings_two = [], []
    for p in range(3):
        d1, d2, _ = ORDERS[p]

        def block_one(i, columns=slice(None), p=p, d2=d2):
            return rows_buf[p].at[i, pos[d2], :, columns]

        def block_two(i, columns=slice(None), p=p):
            return rows_buf[p].at[:, i, :, columns]

        rings_one.append(ring(p, d1, 0, block_one))
        rings_two.append(ring(p, d2, 4, block_two))

    def begin(rings):
        for first, _, _ in rings:
            for copy in first:
                copy.start()

    def turn_round(rings):
        for _, second, waits in rings:
            for i in range(2):
                waits[i]()
                second[i].start()

    def finish(rings):
        for _, _, waits in rings:
            waits[2]()
            waits[3]()

    def drain(rings):
        for first, second, _ in rings:
            for copy in first + second:
                copy.wait_send()

    begin(rings_one)
    for load in loads:
        load.start()
    lax.fori_loop(0, 1, attend, 0)
    turn_round(rings_one)
    lax.fori_loop(1, 3, attend, 0)
    finish(rings_one)
    begin(rings_two)
    lax.fori_loop(3, 6, attend, 0)
    turn_round(rings_two)
    lax.fori_loop(6, 8, attend, 0)

    def chooser(p):
        n = iota((512, TABLE), 0)
        other, which, slot = n // 128, (n // 64) % 2, n % 2
        if p == 0:
            expert = ((pos[0] * 2 + pos[1] // 2) * 4 + other) * 2 + which
        elif p == 1:
            expert = ((pos[0] * 2 + other // 2) * 4 + pos[2]) * 2 + which
        else:
            expert = ((other * 2 + pos[1] // 2) * 4 + pos[2]) * 2 + which
        return jnp.where(iota((512, TABLE), 1) == expert * 2 + slot, 1.0, 0.0).astype(jnp.bfloat16)

    def table_of(p):
        return rows_buf[p][:, :, :, pl.ds(WIDTHS[p], TABLE)].reshape(256, TABLE)

    def columns_of(i):
        return pl.ds(pl.multiple_of(i * LANES, LANES), LANES)

    sent = []

    def send(copy):
        copy.start()
        sent.append(copy)

    local = []
    for p in range(3):
        _, _, d3 = ORDERS[p]
        for wait in rings_two[p][2][2:]:
            wait()
        hot = dot_nt(chooser(p), table_of(p))
        near = (iota((512, 256), 0) % 64) // 2 == iota((512, 256), 1) // 8
        picker = jnp.where(near & (hot != 0.0), 1.0, 0.0).astype(jnp.bfloat16)

        def pick(i, carry, p=p, picker=picker):
            block = rows_buf[p][:, :, :, columns_of(i)].reshape(256, LANES)
            slot_buf[p][:, :, columns_of(i)] = dot(picker, block).astype(jnp.bfloat16).reshape(8, 64, LANES)
            return carry

        lax.fori_loop(0, WIDTHS[p] // LANES, pick, 0)

        here = pos[d3]
        far = (here + 2) % 4
        mine = core * 4 + here
        if d3 != 1:
            for delta in (1, -1):
                there = (here + delta) % 4
                for which in range(2):
                    target = device(moved(d3, delta), which)
                    send(remote(slot_buf[p].at[there * 2 + which], recv_buf[p].at[mine], p, 8 + (delta + 1) + which, 8 + mine, target))
            for which, delta in ((0, 1), (1, -1)):
                target = device(moved(d3, delta), which)
                send(remote(slot_buf[p].at[far * 2 + which], relay_in[p].at[core], p, 12 + which, 16 + core, target))
        else:
            for delta, base in ((-pair, 8), (pair, 10)):
                there = (here + delta) % 4
                for which in range(2):
                    target = device(moved(d3, delta), which)
                    send(remote(slot_buf[p].at[there * 2 + which], recv_buf[p].at[mine], p, base + which, 8 + mine, target))
        send(remote(slot_buf[p].at[here * 2 + 1 - core], recv_buf[p].at[mine], p, 14, 8 + mine, device(pos, 1 - core)))
        local.append(pltpu.make_async_copy(slot_buf[p].at[here * 2 + core], recv_buf[p].at[mine], own_sem.at[3 + p]))
        local[p].start()

    for p in range(3):
        _, _, d3 = ORDERS[p]
        here = pos[d3]
        for c in range(2):
            if d3 != 1:
                arrived(relay_in[p].at[c], p, 16 + c)
                source = (here - turn) % 4
                entry = c * 4 + source
                send(remote(relay_in[p].at[c], recv_buf[p].at[entry], p, 18 + c, 8 + entry, device(moved(d3, turn), core)))
            else:
                source = (here - pair) % 4
                entry = c * 4 + source
                arrived(recv_buf[p].at[entry], p, 8 + entry)
                send(remote(recv_buf[p].at[entry], recv_buf[p].at[entry], p, 18 + c, 8 + entry, device(moved(d3, pair), core)))

    for p in range(3):
        _, _, d3 = ORDERS[p]
        here = pos[d3]
        for c in range(2):
            for delta in (1, 3, 2):
                entry = c * 4 + (here + delta) % 4
                if d3 != 1:
                    arrived(recv_buf[p].at[entry], p, 8 + entry)
        if d3 == 1:
            for c in range(2):
                for delta in (pair, 2):
                    entry = c * 4 + (here + delta) % 4
                    arrived(recv_buf[p].at[entry], p, 8 + entry)
        arrived(recv_buf[p].at[(1 - core) * 4 + here], p, 8 + (1 - core) * 4 + here)
        local[p].wait()
    for copy in sent:
        copy.wait_send()
    drain(rings_one)
    drain(rings_two)
    for step in (6, 7):
        o_copy(step, step % 2).wait()
    for load in loads:
        load.wait()

    def source_row(p, i):
        z, x, y, q = i // 64, (i // 16) % 4, (i // 4) % 4, i % 4
        if p == 1:
            return y * 64 + z * 16 + x * 4 + q
        return x * 64 + y * 16 + z * 4 + q

    acc[...] = jnp.zeros_like(acc)
    for p in range(3):
        held = recv_buf[p]
        if p > 0:
            held = slot_buf[p]
            order = jnp.where(source_row(p, iota((256, 256), 0)) == iota((256, 256), 1), 1.0, 0.0).astype(jnp.bfloat16)

            def straighten(i, carry, p=p, order=order):
                for c in range(2):
                    block = recv_buf[p][pl.ds(c * 4, 4), :, columns_of(i)].reshape(256, LANES)
                    slot_buf[p][pl.ds(c * 4, 4), :, columns_of(i)] = dot(order, block).astype(jnp.bfloat16).reshape(4, 64, LANES)
                return carry

            lax.fori_loop(0, WIDTHS[p] // LANES, straighten, 0)

        def widen(i, carry, p=p, held=held):
            step = STEPS[p]
            start = pl.multiple_of(i * step, 256)
            block = held[:, :, pl.ds(start, step)].reshape(512, step)
            deep = pl.ds(pl.multiple_of(OFFSETS[p] + start, 256), step)
            for n in range(2):
                acc[:, n * 256 : n * 256 + 256] += dot(block, gate_buf[deep, n * 256 : n * 256 + 256])
                acc[:, 512 + n * 256 : 768 + n * 256] += dot(block, up_buf[deep, n * 256 : n * 256 + 256])
            return carry

        lax.fori_loop(0, WIDTHS[p] // STEPS[p], widen, 0)

    def activate(i, carry):
        rows = pl.ds(pl.multiple_of(i * 64, 64), 64)
        gate_val = acc[rows, 0:512]
        hid[rows, :] = ((gate_val / (1.0 + jnp.exp(-gate_val))) * acc[rows, 512:1024]).astype(jnp.bfloat16)
        return carry

    lax.fori_loop(0, 8, activate, 0)

    returned = []

    def give(copy):
        copy.start()
        returned.append(copy)

    for p in range(3):
        _, _, d3 = ORDERS[p]
        if p == 0:
            hid_p[...] = hid[...]
        else:
            order = jnp.where(source_row(p, iota((256, 256), 1)) == iota((256, 256), 0), 1.0, 0.0).astype(jnp.bfloat16)
            for c in range(2):
                hid_p[c * 256 : c * 256 + 256, :] = dot(order, hid[c * 256 : c * 256 + 256, :]).astype(jnp.bfloat16)

        def narrow(i, carry, p=p):
            deep = pl.ds(pl.multiple_of(OFFSETS[p] + i * LANES, LANES), LANES)
            recv_buf[p][:, :, columns_of(i)] = dot(hid_p[...], down_buf[:, deep]).astype(jnp.bfloat16).reshape(8, 64, LANES)
            return carry

        lax.fori_loop(0, WIDTHS[p] // LANES, narrow, 0)

        here = pos[d3]
        far = (here + 2) % 4
        entry = here * 2 + core
        for delta, base in ((1, 20), (-1, 22)):
            there = (here + delta) % 4
            for c in range(2):
                give(remote(recv_buf[p].at[c * 4 + there], back_buf[p].at[entry], p, base + c, 20 + entry, device(moved(d3, delta), c)))
        step = turn if d3 != 1 else pair
        for c in range(2):
            give(remote(recv_buf[p].at[c * 4 + far], relay_out[p].at[c], p, 24 + c, 28 + c, device(moved(d3, step), core)))
        give(remote(recv_buf[p].at[(1 - core) * 4 + here], back_buf[p].at[entry], p, 26, 20 + entry, device(pos, 1 - core)))
        local[p] = pltpu.make_async_copy(recv_buf[p].at[core * 4 + here], back_buf[p].at[entry], own_sem.at[6 + p])
        local[p].start()

    for p in range(3):
        _, _, d3 = ORDERS[p]
        here = pos[d3]
        step = turn if d3 != 1 else -pair
        origin = -turn if d3 != 1 else pair
        entry = ((here + origin) % 4) * 2 + core
        for c in range(2):
            arrived(relay_out[p].at[c], p, 28 + c)
            give(remote(relay_out[p].at[c], back_buf[p].at[entry], p, 28 + c, 20 + entry, device(moved(d3, step), c)))

    def fold(p, dim, base, block, bufs):
        half = HALVES[p]
        rest = WIDTHS[p] - half
        here, up, down, far = pos[dim], (pos[dim] + 1) % 4, (pos[dim] + 3) % 4, (pos[dim] + 2) % 4
        above, below = device(moved(dim, 1), core), device(moved(dim, -1), core)
        low_part = lambda i: block(i, pl.ds(0, half))
        high_part = lambda i: block(i, pl.ds(half, rest))
        first = [
            remote(low_part(far), bufs[0], p, base, base, above),
            remote(high_part(far), bufs[1], p, base + 1, base + 1, below),
        ]
        second = [
            remote(block(up), bufs[2], p, base + 2, base + 2, above),
            remote(block(down), bufs[3], p, base + 3, base + 3, below),
        ]
        return first, second, low_part(up), high_part(down)

    folds_two, folds_one = [], []
    for p in range(3):
        d1, d2, d3 = ORDERS[p]
        here = pos[d3]
        arrivals = [(here * 2 + 1 - core)]
        for delta in (1, 2, 3):
            for which in range(2):
                arrivals.append(((here + delta) % 4) * 2 + which)
        for entry in arrivals:
            arrived(back_buf[p].at[entry], p, 20 + entry)
        local[p].wait()
        near = (iota((256, 512), 1) % 64) // 2 == iota((256, 512), 0) // 8
        mixer = jnp.where(near, dot_nt(table_of(p), chooser(p)), 0.0).astype(jnp.bfloat16)

        def mix(i, carry, p=p, mixer=mixer):
            block = back_buf[p][:, :, columns_of(i)].reshape(512, LANES)
            part_buf[p][:, :, :, columns_of(i)] = dot(mixer, block).astype(jnp.bfloat16).reshape(4, 4, 16, LANES)
            return carry

        lax.fori_loop(0, WIDTHS[p] // LANES, mix, 0)

        def block_two(i, columns=slice(None), p=p):
            return part_buf[p].at[:, i, :, columns]

        def block_one(i, columns=slice(None), p=p, d2=d2):
            return part_buf[p].at[i, pos[d2], :, columns]

        folds_two.append(fold(p, d2, 30, block_two, (wide_a[p], wide_b[p], wide_c[p], wide_d[p])))
        folds_one.append(fold(p, d1, 34, block_one, (thin_a[p], thin_b[p], thin_c[p], thin_d[p])))
        for copy in folds_two[p][0]:
            give(copy)

    def add_into(ref, *others):
        total = ref[...].astype(jnp.float32)
        for other in others:
            total = total + other[...].astype(jnp.float32)
        ref[...] = total.astype(jnp.bfloat16)

    for p in range(3):
        first, second, low_up, high_down = folds_two[p]
        arrived(wide_a[p], p, 30)
        add_into(low_up, wide_a[p])
        give(second[0])
        arrived(wide_b[p], p, 31)
        add_into(high_down, wide_b[p])
        give(second[1])
    for p in range(3):
        d1, d2, d3 = ORDERS[p]
        arrived(wide_c[p], p, 32)
        arrived(wide_d[p], p, 33)
        add_into(part_buf[p].at[:, pos[d2]], wide_c[p], wide_d[p])
        for copy in folds_one[p][0]:
            give(copy)
    for p in range(3):
        first, second, low_up, high_down = folds_one[p]
        arrived(thin_a[p], p, 34)
        add_into(low_up, thin_a[p])
        give(second[0])
        arrived(thin_b[p], p, 35)
        add_into(high_down, thin_b[p])
        give(second[1])
    for p in range(3):
        d1, d2, d3 = ORDERS[p]
        arrived(thin_c[p], p, 36)
        arrived(thin_d[p], p, 37)
        total = part_buf[p][pos[d1], pos[d2]].astype(jnp.float32)
        total = total + thin_c[p][...].astype(jnp.float32) + thin_d[p][...].astype(jnp.float32)
        out_ref[:, pl.ds(OFFSETS[p], WIDTHS[p])] = total.astype(jnp.bfloat16)
    for copy in returned:
        copy.wait_send()


def per_device(
    hidden_in,
    expert_ids,
    gate_coef,
    query_lat,
    kv_cache,
    cache_len,
    gate_weight,
    up_weight,
    down_weight,
):
    bf16, f32 = jnp.bfloat16, jnp.float32
    vmem = lambda *shape, dtype=bf16: pltpu.VMEM(shape, dtype)
    dma = pltpu.SemaphoreType.DMA
    scratch = (
        [vmem(4, 4, 16, w + TABLE) for w in WIDTHS]
        + [vmem(8, 64, w) for w in WIDTHS]
        + [vmem(8, 64, w) for w in WIDTHS]
        + [vmem(8, 64, w) for w in WIDTHS]
        + [vmem(2, 64, w) if i != 1 else vmem(2, 64, 128) for i, w in enumerate(WIDTHS)]
        + [vmem(2, 64, w) for w in WIDTHS]
        + [vmem(4, 4, 16, w) for w in WIDTHS]
        + [vmem(4, 16, h) for h in HALVES]
        + [vmem(4, 16, w - h) for w, h in zip(WIDTHS, HALVES)]
        + [vmem(4, 16, w) for w in WIDTHS]
        + [vmem(4, 16, w) for w in WIDTHS]
        + [vmem(16, h) for h in HALVES]
        + [vmem(16, w - h) for w, h in zip(WIDTHS, HALVES)]
        + [vmem(16, w) for w in WIDTHS]
        + [vmem(16, w) for w in WIDTHS]
        + [
            vmem(7168, 512),
            vmem(7168, 512),
            vmem(512, 7168),
            vmem(512, 1024, dtype=f32),
            vmem(512, 512),
            vmem(512, 512),
            vmem(2, 2, 64, 576),
            vmem(2, 2, 128, 576),
            vmem(2, 2, 64, 512),
            dma((3, 38)),
            dma((3, 38)),
            dma((3,)),
            dma((9,)),
            dma((2,)),
            dma((2,)),
            dma((2,)),
        ]
    )
    anywhere = pl.BlockSpec(memory_space=pl.ANY)
    in_vmem = pl.BlockSpec(memory_space=pltpu.VMEM)
    return pl.pallas_call(
        kernel,
        out_shape=(
            jax.ShapeDtypeStruct((16, 64, 512), bf16),
            jax.ShapeDtypeStruct((16, 7168), bf16),
        ),
        in_specs=[pl.BlockSpec(memory_space=pltpu.SMEM), in_vmem, in_vmem] + [anywhere] * 6,
        out_specs=(anywhere, in_vmem),
        scratch_shapes=scratch,
        compiler_params=pltpu.CompilerParams(
            collective_id=0, has_side_effects=True, vmem_limit_bytes=67043328
        ),
        name="moe_step",
    )(
        cache_len,
        expert_ids,
        gate_coef,
        hidden_in,
        query_lat,
        kv_cache,
        gate_weight,
        up_weight,
        down_weight,
    )


def solution(mesh):
    in_specs = (
        P(("sec", "dev"), None),
        P(("sec", "dev"), None),
        P(("sec", "dev"), None),
        P(("sec", "dev"), None, None),
        P(("sec", "dev"), None, None),
        P(("sec", "dev")),
        P("dev", None, "sec"),
        P("dev", None, "sec"),
        P("dev", "sec", None),
    )
    out_specs = (P(("sec", "dev"), None, None), P(("sec", "dev"), None))
    return jax.shard_map(
        per_device, mesh=mesh, in_specs=in_specs, out_specs=out_specs, check_vma=False
    )
```

time: 307 us -> 165 us (0.54)
  the two profiles are of different devices: /device:TPU:23 before, /device:TPU:0 now
where the time goes in v1:
time: 165 us; the launch traced here: 162 us
  Pallas kernels  150 us (91%)
  local copies, waits for them, and re-layouts  11 us (7%)
    pallas_call x1, Pallas kernels, per_device(): pl.pallas_call(kernel, out_shape=(jax.ShapeDtypeStruct((16, 64, 512), bf1...  150 us
    unnamed x5, local copies, waits for them, and re-layouts  11 us

profile of v1, /device:TPU:0, one launch (start us, length us, event | category | flops | bytes accessed | tf_op | source)
XLA Modules:
  0.0 161.9 jit_solution(7015510981728361423)
XLA Ops:
  0.6 1.4 copy.11.ids_ref
  2.0 1.4 copy.12.coef_ref
  3.3 4.3 %copy.13.cache_ref = bf16[16,128,576]{2,1,0:T(8,128)(2,1)} copy(bf16[16,128,576]{1,2,0:T(8,128)(2,1)} %param.13) | data formatting | bytes 4718592 | tf_op args[4]
  7.7 150.3 %moe_step.1 = (bf16[16,64,512]{2,1,0:T(8,128)(2,1)}, bf16[16,7168]{1,0:T(8,128)(2,1)}) custom-call(s32[16]{0:T(128)} %len_ref.1, s32[16,8]{1,0:T(8,128)} %copy.11.ids_ref, f32[16,8]{1,0:T(8,128)} %copy.12.coef_ref, bf16[16,7168]{1,0:T(8,128)(2,1)} %hidden_ref.1, bf16[16,64,576]{2,1,0:T(8,128)(2,1)} %query_ref.1, bf16[16,128,576]{2,1,0:T(8,128)(2,1)} %copy.13.cache_ref, ...), custom_call_target="tpu_custom_call" | custom-call | tf_op jit(solution)/shard_map/moe_step/pallas_call | solution.py:579
  158.0 2.3 %copy.16 = bf16[16,64,512]{2,1,0:T(8,128)(2,1)} copy(bf16[16,64,512]{2,1,0:T(8,128)(2,1)} %get-tuple-element.4) | data formatting | bytes 2097152
  160.2 1.6 %copy.17 = bf16[16,7168]{1,0:T(8,128)(2,1)} copy(bf16[16,7168]{1,0:T(8,128)(2,1)} %get-tuple-element.5) | data formatting | bytes 458752

commit v2 on v1

v2 whole, which is shorter than its diff:
```python
import functools
import math

import jax
import jax.numpy as jnp
from jax import lax
from jax.experimental import pallas as pl
from jax.experimental.pallas import tpu as pltpu
from jax.sharding import PartitionSpec as P

LAT = 512
TOP = 8
MESH = pl.DeviceIdType.MESH
SCALE = 1.0 / math.sqrt(192.0)

WIDTHS = (1280, 1280, 1024, 1024, 1280, 1280)
OFFSETS = (0, 1280, 2560, 3584, 4608, 5888)
EXTRA = (128, 128, 128, 0, 0, 0)
ORDERS = ((0, 1, 2), (2, 0, 1), (1, 2, 0)) * 2
PIECES = 6
GROUP_A, GROUP_B = (0, 1, 2), (3, 4, 5)
TABLE = 128
LANES = 256


def iota(shape, dim):
    return lax.broadcasted_iota(jnp.int32, shape, dim)


def dot(a, b):
    return jnp.dot(a, b, preferred_element_type=jnp.float32)


def dot_nt(a, b):
    return lax.dot_general(a, b, (((1,), (1,)), ((), ())), preferred_element_type=jnp.float32)


def kernel(
    len_ref,
    ids_ref,
    coef_ref,
    hidden_ref,
    query_ref,
    cache_ref,
    gate_ref,
    up_ref,
    down_ref,
    att_ref,
    out_ref,
    *scratch,
):
    many = [scratch[i * PIECES : (i + 1) * PIECES] for i in range(15)]
    rows_buf, slot_buf, recv_buf, back_buf, relay_in, relay_out, part_buf = many[:7]
    wide_a, wide_b, wide_c, wide_d, thin_a, thin_b, thin_c, thin_d = many[7:]
    (gate_buf, up_buf, down_buf, acc, hid, hid_p, q_buf, kv_buf, o_buf) = scratch[90:99]
    send_sem, recv_sem, load_sem, own_sem, q_sem, kv_sem, o_sem = scratch[99:]

    sec = lax.axis_index("sec")
    dev = lax.axis_index("dev")
    core = dev % 2
    pos = (dev // 16, ((dev // 8) % 2) * 2 + sec, (dev // 2) % 4)

    def device(point, which):
        x, y, z = point
        return (y % 2, ((x * 2 + y // 2) * 4 + z) * 2 + which)

    def moved(dim, delta):
        point = list(pos)
        point[dim] = (pos[dim] + delta) % 4
        return tuple(point)

    turn = 1 - 2 * core
    pair = 1 - 2 * (pos[1] % 2)

    loads = [
        pltpu.make_async_copy(gate_ref.at[0], gate_buf, load_sem.at[0]),
        pltpu.make_async_copy(up_ref.at[0], up_buf, load_sem.at[1]),
        pltpu.make_async_copy(down_ref.at[0], down_buf, load_sem.at[2]),
    ]
    own = []
    for p in range(PIECES):
        d1, d2, _ = ORDERS[p]
        own.append(
            pltpu.make_async_copy(
                hidden_ref.at[:, pl.ds(OFFSETS[p], WIDTHS[p])],
                rows_buf[p].at[pos[d1], pos[d2], :, pl.ds(0, WIDTHS[p])],
                own_sem.at[p],
            )
        )
        own[p].start()

    barrier = pltpu.get_barrier_semaphore()
    partners = [device(pos, 1 - core)]
    for dim in range(3):
        for delta in (1, -1):
            for which in range(2):
                partners.append(device(moved(dim, delta), which))
    for partner in partners:
        pl.semaphore_signal(barrier, inc=1, device_id=partner, device_id_type=MESH)

    eye = jnp.where(iota((16, 16), 0) == iota((16, 16), 1), 1.0, 0.0).astype(jnp.bfloat16)
    names = dot_nt(eye, ids_ref[...].astype(jnp.float32).astype(jnp.bfloat16))
    coefs = dot_nt(eye, coef_ref[...].astype(jnp.bfloat16))
    lane = iota((16, TABLE), 1)
    expert_of = (lane // 2).astype(jnp.float32)
    hit = jnp.zeros((16, TABLE), jnp.float32)
    weight = jnp.zeros((16, TABLE), jnp.float32)
    for k in range(TOP):
        match = names[:, k : k + 1] == expert_of
        hit = hit + jnp.where(match, 1.0, 0.0)
        weight = weight + jnp.where(match, coefs[:, k : k + 1], 0.0)
    low = (iota((16, 16), 1) < iota((16, 16), 0)) & (iota((16, 16), 1) // 8 == iota((16, 16), 0) // 8)
    rank = dot(jnp.where(low, 1.0, 0.0).astype(jnp.bfloat16), hit.astype(jnp.bfloat16))
    table = jnp.where(rank == (lane % 2).astype(jnp.float32), weight, 0.0).astype(jnp.bfloat16)
    for p in GROUP_A:
        d1, d2, _ = ORDERS[p]
        rows_buf[p][pos[d1], pos[d2], :, pl.ds(WIDTHS[p], TABLE)] = table

    for p in range(PIECES):
        own[p].wait()
    pl.semaphore_wait(barrier, len(partners))

    def remote(src, dst, p, send, recv, target):
        return pltpu.make_async_remote_copy(
            src_ref=src,
            dst_ref=dst,
            send_sem=send_sem.at[p, send],
            recv_sem=recv_sem.at[p, recv],
            device_id=target,
            device_id_type=MESH,
        )

    def arrived(dst, p, recv):
        remote(dst, dst, p, 0, recv, device(pos, 1 - core)).wait_recv()

    def q_copy(step, slot):
        return pltpu.make_async_copy(query_ref.at[pl.ds(step * 2, 2)], q_buf.at[slot], q_sem.at[slot])

    def kv_copy(step, slot):
        return pltpu.make_async_copy(cache_ref.at[pl.ds(step * 2, 2)], kv_buf.at[slot], kv_sem.at[slot])

    def o_copy(step, slot):
        return pltpu.make_async_copy(o_buf.at[slot], att_ref.at[pl.ds(step * 2, 2)], o_sem.at[slot])

    def attend(step, carry):
        slot = step % 2
        q_copy(step, slot).wait()
        kv_copy(step, slot).wait()

        @pl.when(step >= 2)
        def _():
            o_copy(step, slot).wait()

        for i in range(2):
            keys = kv_buf[slot, i]
            scores = dot(q_buf[slot, i], keys) * SCALE
            visible = iota((64, 128), 1) < len_ref[step * 2 + i]
            scores = jnp.where(visible, scores, -1e30)
            exponent = jnp.exp(scores - jnp.max(scores, axis=1, keepdims=True))
            weights = (exponent / jnp.sum(exponent, axis=1, keepdims=True)).astype(jnp.bfloat16)
            o_buf[slot, i] = dot_nt(weights, keys[:LAT, :]).astype(jnp.bfloat16)
        o_copy(step, slot).start()

        @pl.when(step + 2 < 8)
        def _():
            q_copy(step + 2, slot).start()
            kv_copy(step + 2, slot).start()

        return carry

    for step in range(2):
        q_copy(step, step).start()
        kv_copy(step, step).start()

    def ring(p, dim, base, block):
        half = WIDTHS[p] // 2
        rest = half + EXTRA[p]
        here, up, down = pos[dim], (pos[dim] + 1) % 4, (pos[dim] + 3) % 4
        above, below = device(moved(dim, 1), core), device(moved(dim, -1), core)
        first = [
            remote(block(here), block(here), p, base, base, above),
            remote(block(here), block(here), p, base + 1, base + 1, below),
        ]
        low_part = lambda i: block(i, pl.ds(0, half))
        high_part = lambda i: block(i, pl.ds(half, rest))
        second = [
            remote(low_part(down), low_part(down), p, base + 2, base + 2, above),
            remote(high_part(up), high_part(up), p, base + 3, base + 3, below),
        ]
        far = (pos[dim] + 2) % 4
        waits = [
            lambda: arrived(block(down), p, base),
            lambda: arrived(block(up), p, base + 1),
            lambda: arrived(low_part(far), p, base + 2),
            lambda: arrived(high_part(far), p, base + 3),
        ]
        return first, second, waits

    rings_one, rings_two = [], []
    for p in range(PIECES):
        d1, d2, _ = ORDERS[p]

        def block_one(i, columns=slice(None), p=p, d2=d2):
            return rows_buf[p].at[i, pos[d2], :, columns]

        def block_two(i, columns=slice(None), p=p):
            return rows_buf[p].at[:, i, :, columns]

        rings_one.append(ring(p, d1, 0, block_one))
        rings_two.append(ring(p, d2, 4, block_two))

    def begin(rings, group):
        for p in group:
            for copy in rings[p][0]:
                copy.start()

    def turn_round(rings, group):
        for p in group:
            _, second, waits = rings[p]
            for i in range(2):
                waits[i]()
                second[i].start()

    def finish(rings, p):
        waits = rings[p][2]
        waits[2]()
        waits[3]()

    def drain(rings):
        for first, second, _ in rings:
            for copy in first + second:
                copy.wait_send()

    def chooser(p):
        n = iota((512, TABLE), 0)
        other, which, slot = n // 128, (n // 64) % 2, n % 2
        if ORDERS[p][2] == 2:
            expert = ((pos[0] * 2 + pos[1] // 2) * 4 + other) * 2 + which
        elif ORDERS[p][2] == 1:
            expert = ((pos[0] * 2 + other // 2) * 4 + pos[2]) * 2 + which
        else:
            expert = ((other * 2 + pos[1] // 2) * 4 + pos[2]) * 2 + which
        return jnp.where(iota((512, TABLE), 1) == expert * 2 + slot, 1.0, 0.0).astype(jnp.bfloat16)

    def table_of(p):
        first = p % 3
        return rows_buf[first][:, :, :, pl.ds(WIDTHS[first], TABLE)].reshape(256, TABLE)

    def columns_of(i):
        return pl.ds(pl.multiple_of(i * LANES, LANES), LANES)

    sent = [[] for _ in range(PIECES)]
    local = [None] * PIECES

    def spread(p):
        _, _, d3 = ORDERS[p]
        finish(rings_two, p)
        hot = dot_nt(chooser(p), table_of(p))
        near = (iota((512, 256), 0) % 64) // 2 == iota((512, 256), 1) // 8
        picker = jnp.where(near & (hot != 0.0), 1.0, 0.0).astype(jnp.bfloat16)

        def pick(i, carry):
            block = rows_buf[p][:, :, :, columns_of(i)].reshape(256, LANES)
            slot_buf[p][:, :, columns_of(i)] = dot(picker, block).astype(jnp.bfloat16).reshape(8, 64, LANES)
            return carry

        lax.fori_loop(0, WIDTHS[p] // LANES, pick, 0)

        def send(copy):
            copy.start()
            sent[p].append(copy)

        here = pos[d3]
        far = (here + 2) % 4
        mine = core * 4 + here
        if d3 != 1:
            for which, delta in ((0, 1), (1, -1)):
                target = device(moved(d3, delta), which)
                send(remote(slot_buf[p].at[far * 2 + which], relay_in[p].at[core], p, 12 + which, 16 + core, target))
            deltas = ((1, 10), (-1, 8))
        else:
            deltas = ((-pair, 8), (pair, 10))
        for delta, base in deltas:
            there = (here + delta) % 4
            for which in range(2):
                target = device(moved(d3, delta), which)
                send(remote(slot_buf[p].at[there * 2 + which], recv_buf[p].at[mine], p, base + which, 8 + mine, target))
        send(remote(slot_buf[p].at[here * 2 + 1 - core], recv_buf[p].at[mine], p, 14, 8 + mine, device(pos, 1 - core)))
        local[p] = pltpu.make_async_copy(slot_buf[p].at[here * 2 + core], recv_buf[p].at[mine], own_sem.at[PIECES + p])
        local[p].start()

    def relay(p):
        _, _, d3 = ORDERS[p]
        here = pos[d3]
        for c in range(2):
            if d3 != 1:
                arrived(relay_in[p].at[c], p, 16 + c)
                entry = c * 4 + (here - turn) % 4
                copy = remote(relay_in[p].at[c], recv_buf[p].at[entry], p, 18 + c, 8 + entry, device(moved(d3, turn), core))
            else:
                entry = c * 4 + (here - pair) % 4
                arrived(recv_buf[p].at[entry], p, 8 + entry)
                copy = remote(recv_buf[p].at[entry], recv_buf[p].at[entry], p, 18 + c, 8 + entry, device(moved(d3, pair), core))
            copy.start()
            sent[p].append(copy)

    def collect(p):
        _, _, d3 = ORDERS[p]
        here = pos[d3]
        for c in range(2):
            for delta in (1, 3, 2) if d3 != 1 else (pair, 2):
                entry = c * 4 + (here + delta) % 4
                arrived(recv_buf[p].at[entry], p, 8 + entry)
        entry = (1 - core) * 4 + here
        arrived(recv_buf[p].at[entry], p, 8 + entry)
        local[p].wait()
        for copy in sent[p]:
            copy.wait_send()

    def source_row(p, i):
        z, x, y, q = i // 64, (i // 16) % 4, (i // 4) % 4, i % 4
        if ORDERS[p][2] == 1:
            return y * 64 + z * 16 + x * 4 + q
        return x * 64 + y * 16 + z * 4 + q

    def widen(p):
        held = recv_buf[p]
        if ORDERS[p][2] != 2:
            held = slot_buf[p]
            order = jnp.where(source_row(p, iota((256, 256), 0)) == iota((256, 256), 1), 1.0, 0.0).astype(jnp.bfloat16)

            def straighten(i, carry):
                for c in range(2):
                    block = recv_buf[p][pl.ds(c * 4, 4), :, columns_of(i)].reshape(256, LANES)
                    slot_buf[p][pl.ds(c * 4, 4), :, columns_of(i)] = dot(order, block).astype(jnp.bfloat16).reshape(4, 64, LANES)
                return carry

            lax.fori_loop(0, WIDTHS[p] // LANES, straighten, 0)
        block = held[...].reshape(512, WIDTHS[p])
        deep = slice(OFFSETS[p], OFFSETS[p] + WIDTHS[p])
        for n in range(2):
            for base, buf in ((0, gate_buf), (512, up_buf)):
                product = dot(block, buf[deep, n * 256 : n * 256 + 256])
                columns = slice(base + n * 256, base + n * 256 + 256)
                if p == 0:
                    acc[:, columns] = product
                else:
                    acc[:, columns] += product

    def activate(i, carry):
        rows = pl.ds(pl.multiple_of(i * 64, 64), 64)
        gate_val = acc[rows, 0:512]
        hid[rows, :] = ((gate_val / (1.0 + jnp.exp(-gate_val))) * acc[rows, 512:1024]).astype(jnp.bfloat16)
        return carry

    begin(rings_one, GROUP_A)
    begin(rings_one, GROUP_B)
    for load in loads:
        load.start()
    lax.fori_loop(0, 1, attend, 0)
    turn_round(rings_one, GROUP_A)
    turn_round(rings_one, GROUP_B)
    lax.fori_loop(1, 2, attend, 0)
    for p in GROUP_A + GROUP_B:
        finish(rings_one, p)
        begin(rings_two, (p,))
    lax.fori_loop(2, 5, attend, 0)
    turn_round(rings_two, GROUP_A)
    lax.fori_loop(5, 7, attend, 0)
    for p in GROUP_A:
        spread(p)
    turn_round(rings_two, GROUP_B)
    lax.fori_loop(7, 8, attend, 0)
    for p in GROUP_A:
        relay(p)
    for p in GROUP_B:
        spread(p)
    loads[0].wait()
    loads[1].wait()
    for p in GROUP_A:
        collect(p)
        widen(p)
        relay(p + 3)
    for p in GROUP_B:
        collect(p)
        widen(p)
    drain(rings_one)
    drain(rings_two)
    for step in (6, 7):
        o_copy(step, step % 2).wait()
    loads[2].wait()
    lax.fori_loop(0, 8, activate, 0)

    returned = []

    def give(copy):
        copy.start()
        returned.append(copy)

    def narrow(p):
        _, _, d3 = ORDERS[p]
        if d3 == 2:
            hid_p[...] = hid[...]
        else:
            order = jnp.where(source_row(p, iota((256, 256), 1)) == iota((256, 256), 0), 1.0, 0.0).astype(jnp.bfloat16)
            for c in range(2):
                hid_p[c * 256 : c * 256 + 256, :] = dot(order, hid[c * 256 : c * 256 + 256, :]).astype(jnp.bfloat16)

        def shrink(i, carry):
            deep = pl.ds(pl.multiple_of(OFFSETS[p] + i * LANES, LANES), LANES)
            recv_buf[p][:, :, columns_of(i)] = dot(hid_p[...], down_buf[:, deep]).astype(jnp.bfloat16).reshape(8, 64, LANES)
            return carry

        lax.fori_loop(0, WIDTHS[p] // LANES, shrink, 0)

        here = pos[d3]
        far = (here + 2) % 4
        entry = here * 2 + core
        step = turn if d3 != 1 else pair
        for c in range(2):
            give(remote(recv_buf[p].at[c * 4 + far], relay_out[p].at[c], p, 24 + c, 28 + c, device(moved(d3, step), core)))
        for delta, base in ((1, 20), (-1, 22)):
            there = (here + delta) % 4
            for c in range(2):
                give(remote(recv_buf[p].at[c * 4 + there], back_buf[p].at[entry], p, base + c, 20 + entry, device(moved(d3, delta), c)))
        give(remote(recv_buf[p].at[(1 - core) * 4 + here], back_buf[p].at[entry], p, 26, 20 + entry, device(pos, 1 - core)))
        local[p] = pltpu.make_async_copy(recv_buf[p].at[core * 4 + here], back_buf[p].at[entry], own_sem.at[2 * PIECES + p])
        local[p].start()

    def relay_back(p):
        _, _, d3 = ORDERS[p]
        here = pos[d3]
        step = turn if d3 != 1 else -pair
        origin = -turn if d3 != 1 else pair
        entry = ((here + origin) % 4) * 2 + core
        for c in range(2):
            arrived(relay_out[p].at[c], p, 28 + c)
            give(remote(relay_out[p].at[c], back_buf[p].at[entry], p, 28 + c, 20 + entry, device(moved(d3, step), c)))

    def fold(p, dim, base, block, bufs):
        half = WIDTHS[p] // 2
        rest = half
        here, up, down, far = pos[dim], (pos[dim] + 1) % 4, (pos[dim] + 3) % 4, (pos[dim] + 2) % 4
        above, below = device(moved(dim, 1), core), device(moved(dim, -1), core)
        low_part = lambda i: block(i, pl.ds(0, half))
        high_part = lambda i: block(i, pl.ds(half, rest))
        first = [
            remote(low_part(far), bufs[0], p, base, base, above),
            remote(high_part(far), bufs[1], p, base + 1, base + 1, below),
        ]
        second = [
            remote(block(up), bufs[2], p, base + 2, base + 2, above),
            remote(block(down), bufs[3], p, base + 3, base + 3, below),
        ]
        return first, second, low_part(up), high_part(down)

    folds_two, folds_one = [None] * PIECES, [None] * PIECES

    def merge(p):
        d1, d2, d3 = ORDERS[p]
        here = pos[d3]
        arrivals = [(here * 2 + 1 - core)]
        for delta in (1, 2, 3):
            for which in range(2):
                arrivals.append(((here + delta) % 4) * 2 + which)
        for entry in arrivals:
            arrived(back_buf[p].at[entry], p, 20 + entry)
        local[p].wait()
        near = (iota((256, 512), 1) % 64) // 2 == iota((256, 512), 0) // 8
        mixer = jnp.where(near, dot_nt(table_of(p), chooser(p)), 0.0).astype(jnp.bfloat16)

        def mix(i, carry):
            block = back_buf[p][:, :, columns_of(i)].reshape(512, LANES)
            part_buf[p][:, :, :, columns_of(i)] = dot(mixer, block).astype(jnp.bfloat16).reshape(4, 4, 16, LANES)
            return carry

        lax.fori_loop(0, WIDTHS[p] // LANES, mix, 0)
        block_two = lambda i, columns=slice(None): part_buf[p].at[:, i, :, columns]
        block_one = lambda i, columns=slice(None): part_buf[p].at[i, pos[d2], :, columns]
        folds_two[p] = fold(p, d2, 30, block_two, (wide_a[p], wide_b[p], wide_c[p], wide_d[p]))
        folds_one[p] = fold(p, d1, 34, block_one, (thin_a[p], thin_b[p], thin_c[p], thin_d[p]))
        for copy in folds_two[p][0]:
            give(copy)

    def add_into(ref, *others):
        total = ref[...].astype(jnp.float32)
        for other in others:
            total = total + other[...].astype(jnp.float32)
        ref[...] = total.astype(jnp.bfloat16)

    def halfway(p, folds, base, low_buf, high_buf):
        _, second, low_up, high_down = folds[p]
        arrived(low_buf[p], p, base)
        add_into(low_up, low_buf[p])
        give(second[0])
        arrived(high_buf[p], p, base + 1)
        add_into(high_down, high_buf[p])
        give(second[1])

    def close_two(p):
        arrived(wide_c[p], p, 32)
        arrived(wide_d[p], p, 33)
        add_into(part_buf[p].at[:, pos[ORDERS[p][1]]], wide_c[p], wide_d[p])
        for copy in folds_one[p][0]:
            give(copy)

    def close_one(p):
        d1, d2, _ = ORDERS[p]
        arrived(thin_c[p], p, 36)
        arrived(thin_d[p], p, 37)
        total = part_buf[p][pos[d1], pos[d2]].astype(jnp.float32)
        total = total + thin_c[p][...].astype(jnp.float32) + thin_d[p][...].astype(jnp.float32)
        out_ref[:, pl.ds(OFFSETS[p], WIDTHS[p])] = total.astype(jnp.bfloat16)

    for p in GROUP_A + GROUP_B:
        narrow(p)
    for p in GROUP_A:
        relay_back(p)
    for p in GROUP_A:
        merge(p)
    for p in GROUP_B:
        relay_back(p)
    for p in GROUP_A:
        halfway(p, folds_two, 30, wide_a, wide_b)
    for p in GROUP_B:
        merge(p)
    for p in GROUP_A:
        close_two(p)
    for p in GROUP_B:
        halfway(p, folds_two, 30, wide_a, wide_b)
    for p in GROUP_A:
        halfway(p, folds_one, 34, thin_a, thin_b)
    for p in GROUP_B:
        close_two(p)
    for p in GROUP_A:
        close_one(p)
    for p in GROUP_B:
        halfway(p, folds_one, 34, thin_a, thin_b)
    for p in GROUP_B:
        close_one(p)
    for copy in returned:
        copy.wait_send()


def per_device(
    hidden_in,
    expert_ids,
    gate_coef,
    query_lat,
    kv_cache,
    cache_len,
    gate_weight,
    up_weight,
    down_weight,
):
    bf16, f32 = jnp.bfloat16, jnp.float32
    vmem = lambda *shape, dtype=bf16: pltpu.VMEM(shape, dtype)
    dma = pltpu.SemaphoreType.DMA
    scratch = (
        [vmem(4, 4, 16, w + e) for w, e in zip(WIDTHS, EXTRA)]
        + [vmem(8, 64, w) for w in WIDTHS]
        + [vmem(8, 64, w) for w in WIDTHS]
        + [vmem(8, 64, w) for w in WIDTHS]
        + [vmem(2, 64, w) if o[2] != 1 else vmem(2, 64, 128) for o, w in zip(ORDERS, WIDTHS)]
        + [vmem(2, 64, w) for w in WIDTHS]
        + [vmem(4, 4, 16, w) for w in WIDTHS]
        + [vmem(4, 16, w // 2) for w in WIDTHS] * 2
        + [vmem(4, 16, w) for w in WIDTHS] * 2
        + [vmem(16, w // 2) for w in WIDTHS] * 2
        + [vmem(16, w) for w in WIDTHS] * 2
        + [
            vmem(7168, 512),
            vmem(7168, 512),
            vmem(512, 7168),
            vmem(512, 1024, dtype=f32),
            vmem(512, 512),
            vmem(512, 512),
            vmem(2, 2, 64, 576),
            vmem(2, 2, 576, 128),
            vmem(2, 2, 64, 512),
            dma((PIECES, 38)),
            dma((PIECES, 38)),
            dma((3,)),
            dma((3 * PIECES,)),
            dma((2,)),
            dma((2,)),
            dma((2,)),
        ]
    )
    anywhere = pl.BlockSpec(memory_space=pl.ANY)
    in_vmem = pl.BlockSpec(memory_space=pltpu.VMEM)
    return pl.pallas_call(
        kernel,
        out_shape=(
            jax.ShapeDtypeStruct((16, 64, 512), bf16),
            jax.ShapeDtypeStruct((16, 7168), bf16),
        ),
        in_specs=[pl.BlockSpec(memory_space=pltpu.SMEM), in_vmem, in_vmem] + [anywhere] * 6,
        out_specs=(anywhere, in_vmem),
        scratch_shapes=scratch,
        compiler_params=pltpu.CompilerParams(
            collective_id=0, has_side_effects=True, vmem_limit_bytes=67043328
        ),
        name="moe_step",
    )(
        cache_len,
        expert_ids.T,
        gate_coef.T,
        hidden_in,
        query_lat,
        jnp.swapaxes(kv_cache, 1, 2),
        gate_weight,
        up_weight,
        down_weight,
    )


def solution(mesh):
    in_specs = (
        P(("sec", "dev"), None),
        P(("sec", "dev"), None),
        P(("sec", "dev"), None),
        P(("sec", "dev"), None, None),
        P(("sec", "dev"), None, None),
        P(("sec", "dev")),
        P("dev", None, "sec"),
        P("dev", None, "sec"),
        P("dev", "sec", None),
    )
    out_specs = (P(("sec", "dev"), None, None), P(("sec", "dev"), None))
    return jax.shard_map(
        per_device, mesh=mesh, in_specs=in_specs, out_specs=out_specs, check_vma=False
    )
```

time: 165 us -> 131 us (0.79); the launches traced: 162 us -> 130 us
  Pallas kernels: 150 us -> 126 us
  local copies, waits for them, and re-layouts: 11 us -> 3.93 us
    pallas_call x1, Pallas kernels: 150 us -> 126 us  [per_device(): pl.pallas_call(kernel, out_shape=(jax.ShapeDtypeStruct((16, 64, 512), bf1...]
    unnamed x5 -> x2, local copies, waits for them, and re-layouts: 11 us -> 3.93 us
where the time goes in v2:
time: 131 us; the launch traced here: 130 us
  Pallas kernels  126 us (96%)
  local copies, waits for them, and re-layouts  3.93 us (3%)
    pallas_call x1, Pallas kernels, per_device(): pl.pallas_call(kernel, out_shape=(jax.ShapeDtypeStruct((16, 64, 512), bf1...  126 us
    unnamed x2, local copies, waits for them, and re-layouts  3.93 us

profile of v2, /device:TPU:0, one launch (start us, length us, event | category | flops | bytes accessed | tf_op | source)
XLA Modules:
  0.0 130.5 jit_solution(12289930182178457306)
XLA Ops:
  0.6 125.9 %moe_step.1 = (bf16[16,64,512]{2,1,0:T(8,128)(2,1)}, bf16[16,7168]{1,0:T(8,128)(2,1)}) custom-call(s32[16]{0:T(128)} %len_ref.1, s32[8,16]{1,0:T(8,128)} %bitcast.4, f32[8,16]{1,0:T(8,128)} %bitcast.5, bf16[16,7168]{1,0:T(8,128)(2,1)} %hidden_ref.1, bf16[16,64,576]{2,1,0:T(8,128)(2,1)} %query_ref.1, bf16[16,576,128]{2,1,0:T(8,128)(2,1)} %bitcast.3, ...), custom_call_target="tpu_custom_call" | custom-call | tf_op jit(solution)/shard_map/moe_step/pallas_call | solution.py:592
  126.5 2.3 %copy.13 = bf16[16,64,512]{2,1,0:T(8,128)(2,1)} copy(bf16[16,64,512]{2,1,0:T(8,128)(2,1)} %get-tuple-element.4) | data formatting | bytes 2097152
  128.8 1.6 %copy.14 = bf16[16,7168]{1,0:T(8,128)(2,1)} copy(bf16[16,7168]{1,0:T(8,128)(2,1)} %get-tuple-element.5) | data formatting | bytes 458752

commit v3 on v2

--- a/solution.py
+++ b/solution.py
@@ -49,11 +49,12 @@
     out_ref,
     *scratch,
 ):
+    len_buf, ids_buf, coef_buf, out_buf, out_sem, small_sem = scratch[106:]
     many = [scratch[i * PIECES : (i + 1) * PIECES] for i in range(15)]
     rows_buf, slot_buf, recv_buf, back_buf, relay_in, relay_out, part_buf = many[:7]
     wide_a, wide_b, wide_c, wide_d, thin_a, thin_b, thin_c, thin_d = many[7:]
     (gate_buf, up_buf, down_buf, acc, hid, hid_p, q_buf, kv_buf, o_buf) = scratch[90:99]
-    send_sem, recv_sem, load_sem, own_sem, q_sem, kv_sem, o_sem = scratch[99:]
+    send_sem, recv_sem, load_sem, own_sem, q_sem, kv_sem, o_sem = scratch[99:106]
 
     sec = lax.axis_index("sec")
     dev = lax.axis_index("dev")
@@ -72,11 +73,22 @@
     turn = 1 - 2 * core
     pair = 1 - 2 * (pos[1] % 2)
 
-    loads = [
-        pltpu.make_async_copy(gate_ref.at[0], gate_buf, load_sem.at[0]),
-        pltpu.make_async_copy(up_ref.at[0], up_buf, load_sem.at[1]),
-        pltpu.make_async_copy(down_ref.at[0], down_buf, load_sem.at[2]),
+    barrier = pltpu.get_barrier_semaphore()
+    partners = [device(pos, 1 - core)]
+    for dim in range(3):
+        for delta in (1, -1):
+            for which in range(2):
+                partners.append(device(moved(dim, delta), which))
+    for partner in partners:
+        pl.semaphore_signal(barrier, inc=1, device_id=partner, device_id_type=MESH)
+
+    small = [
+        pltpu.make_async_copy(ids_ref, ids_buf, small_sem.at[0]),
+        pltpu.make_async_copy(coef_ref, coef_buf, small_sem.at[1]),
+        pltpu.make_async_copy(len_ref, len_buf, small_sem.at[2]),
     ]
+    for copy in small:
+        copy.start()
     own = []
     for p in range(PIECES):
         d1, d2, _ = ORDERS[p]
@@ -88,30 +100,28 @@
             )
         )
         own[p].start()
-
-    barrier = pltpu.get_barrier_semaphore()
-    partners = [device(pos, 1 - core)]
-    for dim in range(3):
-        for delta in (1, -1):
-            for which in range(2):
-                partners.append(device(moved(dim, delta), which))
-    for partner in partners:
-        pl.semaphore_signal(barrier, inc=1, device_id=partner, device_id_type=MESH)
+    loads = [
+        pltpu.make_async_copy(gate_ref.at[0], gate_buf, load_sem.at[0]),
+        pltpu.make_async_copy(up_ref.at[0], up_buf, load_sem.at[1]),
+        pltpu.make_async_copy(down_ref.at[0], down_buf, load_sem.at[2]),
+    ]
+    for copy in small:
+        copy.wait()
 
     eye = jnp.where(iota((16, 16), 0) == iota((16, 16), 1), 1.0, 0.0).astype(jnp.bfloat16)
-    names = dot_nt(eye, ids_ref[...].astype(jnp.float32).astype(jnp.bfloat16))
-    coefs = dot_nt(eye, coef_ref[...].astype(jnp.bfloat16))
+    names = dot_nt(eye, ids_buf[...].astype(jnp.float32).astype(jnp.bfloat16))
+    coefs = dot_nt(eye, coef_buf[...].astype(jnp.bfloat16))
     lane = iota((16, TABLE), 1)
-    expert_of = (lane // 2).astype(jnp.float32)
+    expert_of = (lane >> 1).astype(jnp.float32)
     hit = jnp.zeros((16, TABLE), jnp.float32)
     weight = jnp.zeros((16, TABLE), jnp.float32)
     for k in range(TOP):
         match = names[:, k : k + 1] == expert_of
         hit = hit + jnp.where(match, 1.0, 0.0)
         weight = weight + jnp.where(match, coefs[:, k : k + 1], 0.0)
-    low = (iota((16, 16), 1) < iota((16, 16), 0)) & (iota((16, 16), 1) // 8 == iota((16, 16), 0) // 8)
+    low = (iota((16, 16), 1) < iota((16, 16), 0)) & ((iota((16, 16), 1) >> 3) == (iota((16, 16), 0) >> 3))
     rank = dot(jnp.where(low, 1.0, 0.0).astype(jnp.bfloat16), hit.astype(jnp.bfloat16))
-    table = jnp.where(rank == (lane % 2).astype(jnp.float32), weight, 0.0).astype(jnp.bfloat16)
+    table = jnp.where(rank == (lane & 1).astype(jnp.float32), weight, 0.0).astype(jnp.bfloat16)
     for p in GROUP_A:
         d1, d2, _ = ORDERS[p]
         rows_buf[p][pos[d1], pos[d2], :, pl.ds(WIDTHS[p], TABLE)] = table
@@ -154,7 +164,7 @@
         for i in range(2):
             keys = kv_buf[slot, i]
             scores = dot(q_buf[slot, i], keys) * SCALE
-            visible = iota((64, 128), 1) < len_ref[step * 2 + i]
+            visible = iota((64, 128), 1) < len_buf[step * 2 + i]
             scores = jnp.where(visible, scores, -1e30)
             exponent = jnp.exp(scores - jnp.max(scores, axis=1, keepdims=True))
             weights = (exponent / jnp.sum(exponent, axis=1, keepdims=True)).astype(jnp.bfloat16)
@@ -233,11 +243,11 @@
 
     def chooser(p):
         n = iota((512, TABLE), 0)
-        other, which, slot = n // 128, (n // 64) % 2, n % 2
+        other, which, slot = n >> 7, (n >> 6) & 1, n & 1
         if ORDERS[p][2] == 2:
             expert = ((pos[0] * 2 + pos[1] // 2) * 4 + other) * 2 + which
         elif ORDERS[p][2] == 1:
-            expert = ((pos[0] * 2 + other // 2) * 4 + pos[2]) * 2 + which
+            expert = ((pos[0] * 2 + (other >> 1)) * 4 + pos[2]) * 2 + which
         else:
             expert = ((other * 2 + pos[1] // 2) * 4 + pos[2]) * 2 + which
         return jnp.where(iota((512, TABLE), 1) == expert * 2 + slot, 1.0, 0.0).astype(jnp.bfloat16)
@@ -256,7 +266,7 @@
         _, _, d3 = ORDERS[p]
         finish(rings_two, p)
         hot = dot_nt(chooser(p), table_of(p))
-        near = (iota((512, 256), 0) % 64) // 2 == iota((512, 256), 1) // 8
+        near = ((iota((512, 256), 0) & 63) >> 1) == (iota((512, 256), 1) >> 3)
         picker = jnp.where(near & (hot != 0.0), 1.0, 0.0).astype(jnp.bfloat16)
 
         def pick(i, carry):
@@ -318,7 +328,7 @@
             copy.wait_send()
 
     def source_row(p, i):
-        z, x, y, q = i // 64, (i // 16) % 4, (i // 4) % 4, i % 4
+        z, x, y, q = i >> 6, (i >> 4) & 3, (i >> 2) & 3, i & 3
         if ORDERS[p][2] == 1:
             return y * 64 + z * 16 + x * 4 + q
         return x * 64 + y * 16 + z * 4 + q
@@ -366,11 +376,11 @@
         begin(rings_two, (p,))
     lax.fori_loop(2, 5, attend, 0)
     turn_round(rings_two, GROUP_A)
-    lax.fori_loop(5, 7, attend, 0)
+    lax.fori_loop(5, 6, attend, 0)
+    turn_round(rings_two, GROUP_B)
     for p in GROUP_A:
         spread(p)
-    turn_round(rings_two, GROUP_B)
-    lax.fori_loop(7, 8, attend, 0)
+    lax.fori_loop(6, 8, attend, 0)
     for p in GROUP_A:
         relay(p)
     for p in GROUP_B:
@@ -413,6 +423,8 @@
 
         lax.fori_loop(0, WIDTHS[p] // LANES, shrink, 0)
 
+    def send_back(p):
+        _, _, d3 = ORDERS[p]
         here = pos[d3]
         far = (here + 2) % 4
         entry = here * 2 + core
@@ -466,7 +478,7 @@
         for entry in arrivals:
             arrived(back_buf[p].at[entry], p, 20 + entry)
         local[p].wait()
-        near = (iota((256, 512), 1) % 64) // 2 == iota((256, 512), 0) // 8
+        near = ((iota((256, 512), 1) & 63) >> 1) == (iota((256, 512), 0) >> 3)
         mixer = jnp.where(near, dot_nt(table_of(p), chooser(p)), 0.0).astype(jnp.bfloat16)
 
         def mix(i, carry):
@@ -504,18 +516,28 @@
         for copy in folds_one[p][0]:
             give(copy)
 
+    outs = []
+
     def close_one(p):
         d1, d2, _ = ORDERS[p]
         arrived(thin_c[p], p, 36)
         arrived(thin_d[p], p, 37)
         total = part_buf[p][pos[d1], pos[d2]].astype(jnp.float32)
         total = total + thin_c[p][...].astype(jnp.float32) + thin_d[p][...].astype(jnp.float32)
-        out_ref[:, pl.ds(OFFSETS[p], WIDTHS[p])] = total.astype(jnp.bfloat16)
-
-    for p in GROUP_A + GROUP_B:
+        columns = pl.ds(OFFSETS[p], WIDTHS[p])
+        out_buf[:, columns] = total.astype(jnp.bfloat16)
+        outs.append(pltpu.make_async_copy(out_buf.at[:, columns], out_ref.at[:, columns], out_sem.at[p]))
+        outs[-1].start()
+
+    for p in GROUP_A:
         narrow(p)
+        send_back(p)
+    for p in GROUP_B:
+        narrow(p)
     for p in GROUP_A:
         relay_back(p)
+    for p in GROUP_B:
+        send_back(p)
     for p in GROUP_A:
         merge(p)
     for p in GROUP_B:
@@ -538,8 +560,26 @@
         halfway(p, folds_one, 34, thin_a, thin_b)
     for p in GROUP_B:
         close_one(p)
+    for copy in outs:
+        copy.wait()
     for copy in returned:
         copy.wait_send()
+
+
+def hand_over(att_in, out_in, att_out, out_out, att_buf, out_buf, in_sem, out_sem):
+    parts = [(out_in, out_buf, out_out)]
+    for i in range(4):
+        rows = pl.ds(i * 4, 4)
+        parts.append((att_in.at[rows], att_buf.at[rows], att_out.at[rows]))
+    takes = [pltpu.make_async_copy(a, b, in_sem.at[i]) for i, (a, b, _) in enumerate(parts)]
+    gives = [pltpu.make_async_copy(b, c, out_sem.at[i]) for i, (_, b, c) in enumerate(parts)]
+    for take in takes:
+        take.start()
+    for take, give in zip(takes, gives):
+        take.wait()
+        give.start()
+    for give in gives:
+        give.wait()
 
 
 def per_device(
@@ -585,18 +625,23 @@
             dma((2,)),
             dma((2,)),
             dma((2,)),
+            pltpu.SMEM((16,), jnp.int32),
+            vmem(8, 16, dtype=jnp.int32),
+            vmem(8, 16, dtype=f32),
+            vmem(16, 7168),
+            dma((PIECES,)),
+            dma((3,)),
         ]
     )
     anywhere = pl.BlockSpec(memory_space=pl.ANY)
-    in_vmem = pl.BlockSpec(memory_space=pltpu.VMEM)
-    return pl.pallas_call(
+    attention, routed = pl.pallas_call(
         kernel,
         out_shape=(
             jax.ShapeDtypeStruct((16, 64, 512), bf16),
             jax.ShapeDtypeStruct((16, 7168), bf16),
         ),
-        in_specs=[pl.BlockSpec(memory_space=pltpu.SMEM), in_vmem, in_vmem] + [anywhere] * 6,
-        out_specs=(anywhere, in_vmem),
+        in_specs=[anywhere] * 9,
+        out_specs=(anywhere, anywhere),
         scratch_shapes=scratch,
         compiler_params=pltpu.CompilerParams(
             collective_id=0, has_side_effects=True, vmem_limit_bytes=67043328
@@ -613,6 +658,17 @@
         up_weight,
         down_weight,
     )
+    return pl.pallas_call(
+        hand_over,
+        out_shape=(
+            jax.ShapeDtypeStruct((16, 64, 512), bf16),
+            jax.ShapeDtypeStruct((16, 7168), bf16),
+        ),
+        in_specs=[anywhere] * 2,
+        out_specs=(anywhere, anywhere),
+        scratch_shapes=[vmem(16, 64, 512), vmem(16, 7168), dma((5,)), dma((5,))],
+        name="hand_over",
+    )(attention, routed)
 
 
 def solution(mesh):

time: 131 us -> 127 us (0.969)
  local copies, waits for them, and re-layouts: 3.93 us -> 0 us
    unnamed x2 -> x0, local copies, waits for them, and re-layouts: 3.93 us -> none
    pallas_call x1, Pallas kernels: 126 us -> 124 us  [per_device(): pl.pallas_call(kernel, out_shape=(jax.ShapeDtypeStruct((16, 64, 512), bf1...]
    pallas_call x0 -> x1, Pallas kernels: none -> 2.12 us  [per_device(): pl.pallas_call(hand_over, out_shape=(jax.ShapeDtypeStruct((16, 64, 512),...]
where the time goes in v3:
time: 127 us
  Pallas kernels  126 us (99%)
    pallas_call x1, Pallas kernels, per_device(): pl.pallas_call(kernel, out_shape=(jax.ShapeDtypeStruct((16, 64, 512), bf1...  124 us

profile of v3, /device:TPU:0, one launch (start us, length us, event | category | flops | bytes accessed | tf_op | source)
XLA Modules:
  0.0 126.6 jit_solution(15846897735015303195)
XLA Ops:
  0.6 123.7 %moe_step.1 = (bf16[16,64,512]{2,1,0:T(8,128)(2,1)}, bf16[16,7168]{1,0:T(8,128)(2,1)}) custom-call(s32[16]{0:T(128)} %len_ref.1, s32[8,16]{1,0:T(8,128)} %bitcast.4, f32[8,16]{1,0:T(8,128)} %bitcast.5, bf16[16,7168]{1,0:T(8,128)(2,1)} %hidden_ref.1, bf16[16,64,576]{2,1,0:T(8,128)(2,1)} %query_ref.1, bf16[16,576,128]{2,1,0:T(8,128)(2,1)} %bitcast.3, ...), custom_call_target="tpu_custom_call" | custom-call | tf_op jit(solution)/shard_map/moe_step/pallas_call | solution.py:637
  124.3 2.1 %hand_over.1 = (bf16[16,64,512]{2,1,0:T(8,128)(2,1)}, bf16[16,7168]{1,0:T(8,128)(2,1)}) custom-call(bf16[16,64,512]{2,1,0:T(8,128)(2,1)} %get-tuple-element.4.att_in, bf16[16,7168]{1,0:T(8,128)(2,1)} %get-tuple-element.5.out_in), custom_call_target="tpu_custom_call" | custom-call | tf_op jit(solution)/shard_map/hand_over/pallas_call | solution.py:661

commit v4 on v3

--- a/solution.py
+++ b/solution.py
@@ -182,25 +182,29 @@
         q_copy(step, step).start()
         kv_copy(step, step).start()
 
-    def ring(p, dim, base, block):
+    def ring(p, dim, base, late, block):
         half = WIDTHS[p] // 2
         rest = half + EXTRA[p]
         here, up, down = pos[dim], (pos[dim] + 1) % 4, (pos[dim] + 3) % 4
         above, below = device(moved(dim, 1), core), device(moved(dim, -1), core)
-        first = [
-            remote(block(here), block(here), p, base, base, above),
-            remote(block(here), block(here), p, base + 1, base + 1, below),
-        ]
         low_part = lambda i: block(i, pl.ds(0, half))
         high_part = lambda i: block(i, pl.ds(half, rest))
+        first = [
+            remote(low_part(here), low_part(here), p, base, base, above),
+            remote(high_part(here), high_part(here), p, base + 1, base + 1, below),
+            remote(high_part(here), high_part(here), p, late, late, above),
+            remote(low_part(here), low_part(here), p, late + 1, late + 1, below),
+        ]
         second = [
             remote(low_part(down), low_part(down), p, base + 2, base + 2, above),
             remote(high_part(up), high_part(up), p, base + 3, base + 3, below),
         ]
         far = (pos[dim] + 2) % 4
         waits = [
-            lambda: arrived(block(down), p, base),
-            lambda: arrived(block(up), p, base + 1),
+            lambda: arrived(low_part(down), p, base),
+            lambda: arrived(high_part(up), p, base + 1),
+            lambda: arrived(high_part(down), p, late),
+            lambda: arrived(low_part(up), p, late + 1),
             lambda: arrived(low_part(far), p, base + 2),
             lambda: arrived(high_part(far), p, base + 3),
         ]
@@ -216,8 +220,8 @@
         def block_two(i, columns=slice(None), p=p):
             return rows_buf[p].at[:, i, :, columns]
 
-        rings_one.append(ring(p, d1, 0, block_one))
-        rings_two.append(ring(p, d2, 4, block_two))
+        rings_one.append(ring(p, d1, 0, 38, block_one))
+        rings_two.append(ring(p, d2, 4, 40, block_two))
 
     def begin(rings, group):
         for p in group:
@@ -233,8 +237,8 @@
 
     def finish(rings, p):
         waits = rings[p][2]
-        waits[2]()
-        waits[3]()
+        for wait in waits[2:]:
+            wait()
 
     def drain(rings):
         for first, second, _ in rings:
@@ -394,10 +398,6 @@
     for p in GROUP_B:
         collect(p)
         widen(p)
-    drain(rings_one)
-    drain(rings_two)
-    for step in (6, 7):
-        o_copy(step, step % 2).wait()
     loads[2].wait()
     lax.fori_loop(0, 8, activate, 0)
 
@@ -449,7 +449,13 @@
             arrived(relay_out[p].at[c], p, 28 + c)
             give(remote(relay_out[p].at[c], back_buf[p].at[entry], p, 28 + c, 20 + entry, device(moved(d3, step), c)))
 
-    def fold(p, dim, base, block, bufs):
+    def low_of(p, ref):
+        return ref.at[(slice(None),) * (len(ref.shape) - 1) + (pl.ds(0, WIDTHS[p] // 2),)]
+
+    def high_of(p, ref):
+        return ref.at[(slice(None),) * (len(ref.shape) - 1) + (pl.ds(WIDTHS[p] // 2, WIDTHS[p] // 2),)]
+
+    def fold(p, dim, base, late, block, bufs):
         half = WIDTHS[p] // 2
         rest = half
         here, up, down, far = pos[dim], (pos[dim] + 1) % 4, (pos[dim] + 3) % 4, (pos[dim] + 2) % 4
@@ -459,10 +465,12 @@
         first = [
             remote(low_part(far), bufs[0], p, base, base, above),
             remote(high_part(far), bufs[1], p, base + 1, base + 1, below),
+            remote(high_part(up), high_of(p, bufs[2]), p, late, late, above),
+            remote(low_part(down), low_of(p, bufs[3]), p, late + 1, late + 1, below),
         ]
         second = [
-            remote(block(up), bufs[2], p, base + 2, base + 2, above),
-            remote(block(down), bufs[3], p, base + 3, base + 3, below),
+            remote(low_part(up), low_of(p, bufs[2]), p, base + 2, base + 2, above),
+            remote(high_part(down), high_of(p, bufs[3]), p, base + 3, base + 3, below),
         ]
         return first, second, low_part(up), high_part(down)
 
@@ -489,8 +497,8 @@
         lax.fori_loop(0, WIDTHS[p] // LANES, mix, 0)
         block_two = lambda i, columns=slice(None): part_buf[p].at[:, i, :, columns]
         block_one = lambda i, columns=slice(None): part_buf[p].at[i, pos[d2], :, columns]
-        folds_two[p] = fold(p, d2, 30, block_two, (wide_a[p], wide_b[p], wide_c[p], wide_d[p]))
-        folds_one[p] = fold(p, d1, 34, block_one, (thin_a[p], thin_b[p], thin_c[p], thin_d[p]))
+        folds_two[p] = fold(p, d2, 30, 42, block_two, (wide_a[p], wide_b[p], wide_c[p], wide_d[p]))
+        folds_one[p] = fold(p, d1, 34, 44, block_one, (thin_a[p], thin_b[p], thin_c[p], thin_d[p]))
         for copy in folds_two[p][0]:
             give(copy)
 
@@ -509,9 +517,14 @@
         add_into(high_down, high_buf[p])
         give(second[1])
 
+    def gather_sums(p, from_below, from_above, base, late):
+        arrived(high_of(p, from_below), p, late)
+        arrived(low_of(p, from_above), p, late + 1)
+        arrived(low_of(p, from_below), p, base + 2)
+        arrived(high_of(p, from_above), p, base + 3)
+
     def close_two(p):
-        arrived(wide_c[p], p, 32)
-        arrived(wide_d[p], p, 33)
+        gather_sums(p, wide_c[p], wide_d[p], 30, 42)
         add_into(part_buf[p].at[:, pos[ORDERS[p][1]]], wide_c[p], wide_d[p])
         for copy in folds_one[p][0]:
             give(copy)
@@ -520,8 +533,7 @@
 
     def close_one(p):
         d1, d2, _ = ORDERS[p]
-        arrived(thin_c[p], p, 36)
-        arrived(thin_d[p], p, 37)
+        gather_sums(p, thin_c[p], thin_d[p], 34, 44)
         total = part_buf[p][pos[d1], pos[d2]].astype(jnp.float32)
         total = total + thin_c[p][...].astype(jnp.float32) + thin_d[p][...].astype(jnp.float32)
         columns = pl.ds(OFFSETS[p], WIDTHS[p])
@@ -538,32 +550,42 @@
         relay_back(p)
     for p in GROUP_B:
         send_back(p)
+    drain(rings_one)
+    drain(rings_two)
+    for step in (6, 7):
+        o_copy(step, step % 2).wait()
     for p in GROUP_A:
         merge(p)
     for p in GROUP_B:
         relay_back(p)
+    slots_sent = len(returned)
     for p in GROUP_A:
         halfway(p, folds_two, 30, wide_a, wide_b)
     for p in GROUP_B:
         merge(p)
     for p in GROUP_A:
         close_two(p)
+    for copy in returned[:slots_sent]:
+        copy.wait_send()
     for p in GROUP_B:
         halfway(p, folds_two, 30, wide_a, wide_b)
+    sums_sent = len(returned)
     for p in GROUP_A:
         halfway(p, folds_one, 34, thin_a, thin_b)
     for p in GROUP_B:
         close_two(p)
+    for copy in returned[slots_sent:sums_sent]:
+        copy.wait_send()
     for p in GROUP_A:
         close_one(p)
     for p in GROUP_B:
         halfway(p, folds_one, 34, thin_a, thin_b)
     for p in GROUP_B:
         close_one(p)
+    for copy in returned[sums_sent:]:
+        copy.wait_send()
     for copy in outs:
         copy.wait()
-    for copy in returned:
-        copy.wait_send()
 
 
 def hand_over(att_in, out_in, att_out, out_out, att_buf, out_buf, in_sem, out_sem):
@@ -618,8 +640,8 @@
             vmem(2, 2, 64, 576),
             vmem(2, 2, 576, 128),
             vmem(2, 2, 64, 512),
-            dma((PIECES, 38)),
-            dma((PIECES, 38)),
+            dma((PIECES, 46)),
+            dma((PIECES, 46)),
             dma((3,)),
             dma((3 * PIECES,)),
             dma((2,)),

time: 127 us -> 126 us (level)
  no operation moved by 1% of the time
where the time goes in v4:
time: 126 us
  Pallas kernels  125 us (99%)
    pallas_call x1, Pallas kernels, per_device(): pl.pallas_call(kernel, out_shape=(jax.ShapeDtypeStruct((16, 64, 512), bf1...  123 us

profile of v4, /device:TPU:0, one launch (start us, length us, event | category | flops | bytes accessed | tf_op | source)
XLA Modules:
  0.0 125.7 jit_solution(936554809789488394)
XLA Ops:
  0.6 122.8 %moe_step.1 = (bf16[16,64,512]{2,1,0:T(8,128)(2,1)}, bf16[16,7168]{1,0:T(8,128)(2,1)}) custom-call(s32[16]{0:T(128)} %len_ref.1, s32[8,16]{1,0:T(8,128)} %bitcast.4, f32[8,16]{1,0:T(8,128)} %bitcast.5, bf16[16,7168]{1,0:T(8,128)(2,1)} %hidden_ref.1, bf16[16,64,576]{2,1,0:T(8,128)(2,1)} %query_ref.1, bf16[16,576,128]{2,1,0:T(8,128)(2,1)} %bitcast.3, ...), custom_call_target="tpu_custom_call" | custom-call | tf_op jit(solution)/shard_map/moe_step/pallas_call | solution.py:659
  123.4 2.1 %hand_over.1 = (bf16[16,64,512]{2,1,0:T(8,128)(2,1)}, bf16[16,7168]{1,0:T(8,128)(2,1)}) custom-call(bf16[16,64,512]{2,1,0:T(8,128)(2,1)} %get-tuple-element.4.att_in, bf16[16,7168]{1,0:T(8,128)(2,1)} %get-tuple-element.5.out_in), custom_call_target="tpu_custom_call" | custom-call | tf_op jit(solution)/shard_map/hand_over/pallas_call | solution.py:683
